TPU v7x, 32 devices: a whole 2x2x4 slice. The times are simulated.
32 devices in a mesh: node: 8 (over z, x), rep: 4 (over y, core).
Axes of the slice: x: 2, y: 2, z: 4, core: 2. Of those that a mesh axis runs over, the one named last changes fastest.
Arguments:
- features: bfloat16 [8192, 512], P(('node', 'rep')), may hold values from -6 to 6
- weight: bfloat16 [512, 512], replicated, may hold values from -0.25 to 0.25
- cotangent: bfloat16 [8192, 512], P(('node', 'rep')), may hold values from -6 to 6
- tile_values: bfloat16 [8192, 128, 128], P(('node', 'rep')), may hold values from -0.125 to 0.125
- tile_row: int32 [8192], P(('node', 'rep')), may hold values from 0 to 7
- tile_col: int32 [8192], P(('node', 'rep')), may hold values from 0 to 15
- tile_count: int32 [32], P(('node', 'rep')), may hold values from 64 to 256, as said below
Outputs:
- activation: bfloat16 [8192, 512], P(('node', 'rep'))
- weight_grad: float32 [512, 512], replicated
- feature_grad: bfloat16 [8192, 512], P(('node', 'rep'))
Inputs may be any that keep to these rules, and one draw needn't show every extreme that they name: `tile_count`: slots of a device below its count hold tiles, the others are ignored; some device uses all 256 slots.
All inputs are finite; a program needn't handle non-finite values.
Results may differ from a plain program's by a relative error of at most 0.023.
Values may be sent and summed in bfloat16 or wider, within the bound.
A program may use at most 128 MiB of HBM per device.

v0:
```python
import math
import jax
import jax.numpy as jnp
from jax import lax
from jax.sharding import PartitionSpec as P

TB = 128


def smooth_gate(values):
    return jax.nn.gelu(values, approximate=True)


def apply_tiles(
    tile_values, tile_row, tile_col, tile_count, sources, target_shape, backward, window_start
):
    group_size = min(32, tile_row.shape[0])
    filled = tile_count[0]
    turns_needed = (filled + group_size - 1) // group_size
    window_blocks = target_shape[0]

    def one_turn(turn_index, totals):
        offset = turn_index * group_size
        values = lax.dynamic_slice_in_dim(tile_values, offset, group_size, 0)
        rows_here = lax.dynamic_slice_in_dim(tile_row, offset, group_size, 0)
        cols_here = lax.dynamic_slice_in_dim(tile_col, offset, group_size, 0)
        slot_mask = (offset + jnp.arange(group_size, dtype=jnp.int32) < filled).astype(jnp.float32)
        if backward:
            local_cols = cols_here - window_start
            inside = ((local_cols >= 0) & (local_cols < window_blocks)).astype(jnp.float32)
            placed = jnp.clip(local_cols, 0, window_blocks - 1)
            product = jnp.einsum(
                "tji,tjf->tif", values, sources[rows_here], preferred_element_type=jnp.float32
            )
            return totals.at[placed].add(product * (slot_mask * inside)[:, None, None])
        product = jnp.einsum(
            "tij,tjf->tif", values, sources[cols_here], preferred_element_type=jnp.float32
        )
        return totals.at[rows_here].add(product * slot_mask[:, None, None])

    return lax.fori_loop(0, turns_needed, one_turn, jnp.zeros(target_shape, jnp.float32))


def local(features, weight, cotangent, tile_values, tile_row, tile_col, tile_count):
    rows_quarter = features.shape[0]
    feature_width = features.shape[1]
    rep_count = lax.axis_size("rep")
    node_count = lax.axis_size("node")
    scale = 1.0 / math.sqrt(rows_quarter * rep_count * node_count)
    gathered = lax.all_gather(features, "node", axis=0, tiled=True)
    source_blocks = gathered.reshape(-1, TB, feature_width)
    block_count = rows_quarter * rep_count // TB
    partial_value = apply_tiles(
        tile_values,
        tile_row,
        tile_col,
        tile_count,
        source_blocks,
        (block_count, TB, feature_width),
        False,
        0,
    ).reshape(block_count * TB, feature_width)
    aggregate_all = lax.psum(partial_value, "rep").astype(jnp.bfloat16)
    cotangent_all = lax.all_gather(cotangent, "rep", axis=0, tiled=True)
    pre = jnp.dot(aggregate_all, weight, preferred_element_type=jnp.float32)
    activated, pullback = jax.vjp(smooth_gate, pre)
    grad_all = pullback(cotangent_all.astype(jnp.float32))[0].astype(jnp.bfloat16)
    full_grad = jnp.dot(grad_all, weight.T, preferred_element_type=jnp.float32).astype(jnp.bfloat16)
    offset = lax.axis_index("rep") * rows_quarter
    own_aggregate = lax.dynamic_slice_in_dim(aggregate_all, offset, rows_quarter, 0)
    own_grad = lax.dynamic_slice_in_dim(grad_all, offset, rows_quarter, 0)
    weight_term = jnp.dot(own_aggregate.T, own_grad, preferred_element_type=jnp.float32)
    output_rows = lax.dynamic_slice_in_dim(activated, offset, rows_quarter, 0).astype(jnp.bfloat16)
    weight_grad = lax.psum(weight_term, ("node", "rep")) * scale
    grad_blocks = full_grad.reshape(block_count, TB, feature_width)
    contributions = apply_tiles(
        tile_values, tile_row, tile_col, tile_count, grad_blocks, source_blocks.shape, True, 0
    )
    feature_grad = lax.psum_scatter(
        contributions.reshape(-1, feature_width).astype(jnp.bfloat16),
        "node",
        scatter_dimension=0,
        tiled=True,
    )
    return (output_rows, weight_grad, feature_grad)


def solution(mesh):
    in_specs = (
        P(("node", "rep"), None),
        P(),
        P(("node", "rep"), None),
        P(("node", "rep"), None, None),
        P(("node", "rep")),
        P(("node", "rep")),
        P(("node", "rep")),
    )
    out_specs = (P(("node", "rep"), None), P(), P(("node", "rep"), None))
    return jax.shard_map(local, mesh=mesh, in_specs=in_specs, out_specs=out_specs, check_vma=False)
```

profile of v0, /device:TPU:0, one launch (start us, length us, event | category | flops | bytes accessed | tf_op | source)
XLA Modules:
  0.0 611.5 jit_solution(17007301135434615890)
XLA Ops:
  9.4 52.6 %all-gather.3.cloned.1.call-done = bf16[2048,512]{1,0:T(8,128)(2,1)} async-done(((bf16[256,512]{1,0:T(8,128)(2,1)}), bf16[2048,512]{1,0:T(8,128)(2,1)}) %all-gather.3.cloned.1.call-update) | async-done | bytes 2097168 | tf_op jit(solution)/shard_map/all_gather | solution.py:50
  62.3 95.9 %while.20 = (s32[]{:T(128)}, f32[8,128,512]{2,1,0:T(8,128)S(1)}, s32[]{:T(128)}, s32[256]{0:T(256)S(1)}, bf16[256,128,128]{2,1,0:T(8,128)(2,1)}, /*index=5*/s32[...) while((s32[]{:T(128)}, f32[8,128,512]{2,1,0:T(8,128)S(1)}, ...), condition=%wide.region_2.3_spmd, body=%wide.region_0.2_spmd.sunk | while | flops 541066560 | bytes 47191344 | solution.py:41
  63.0 4.4 gather_fusion
  67.4 7.2 %broadcast_multiply_fusion.5 = f32[32,128,512]{2,1,0:T(8,128)} fusion(f32[32]{0:T(128)S(1)} %compare_convert_fusion.3, bf16[32,128,512]{2,1,0:T(8,128)(2,1)} %gather_fusion, bf16[256,128,128]{2,1,0:T(8,128)(2,1)} %get-tuple-element.274, s32[]{:T(128)S(6)} %select_n.44), kind=kOutput, calls=%fused_computation.4.clone.1 | convolution fusion | flops 538968064 | bytes 13631620 | tf_op jit(solution)/shard_map/while/body/tij,tjf->tif/dot_general | solution.py:36
  74.6 11.8 %scatter_fusion = f32[8,128,512]{2,1,0:T(8,128)S(1)} fusion(f32[8,128,512]{2,1,0:T(8,128)S(1)} %get-tuple-element.259, s32[32]{0:T(128)S(1)} %get-tuple-element.234, f32[32,128,512]{2,1,0:T(8,128)} %broadcast_multiply_fusion.5), kind=kCustom, calls=%fused_computation.2.clone.1 | custom fusion | flops 2097152 | bytes 25165952 | tf_op jit(solution)/shard_map/while/body/scatter-add | solution.py:39
  91.5 7.0 %broadcast_multiply_fusion.5 = f32[32,128,512]{2,1,0:T(8,128)} fusion(f32[32]{0:T(128)S(1)} %compare_convert_fusion.3, bf16[32,128,512]{2,1,0:T(8,128)(2,1)} %gather_fusion, bf16[256,128,128]{2,1,0:T(8,128)(2,1)} %get-tuple-element.274, s32[]{:T(128)S(6)} %select_n.44), kind=kOutput, calls=%fused_computation.4.clone.1 | convolution fusion | flops 538968064 | bytes 13631620 | tf_op jit(solution)/shard_map/while/body/tij,tjf->tif/dot_general | solution.py:36
  98.5 11.8 %scatter_fusion = f32[8,128,512]{2,1,0:T(8,128)S(1)} fusion(f32[8,128,512]{2,1,0:T(8,128)S(1)} %get-tuple-element.259, s32[32]{0:T(128)S(1)} %get-tuple-element.234, f32[32,128,512]{2,1,0:T(8,128)} %broadcast_multiply_fusion.5), kind=kCustom, calls=%fused_computation.2.clone.1 | custom fusion | flops 2097152 | bytes 25165952 | tf_op jit(solution)/shard_map/while/body/scatter-add | solution.py:39
  115.4 7.0 %broadcast_multiply_fusion.5 = f32[32,128,512]{2,1,0:T(8,128)} fusion(f32[32]{0:T(128)S(1)} %compare_convert_fusion.3, bf16[32,128,512]{2,1,0:T(8,128)(2,1)} %gather_fusion, bf16[256,128,128]{2,1,0:T(8,128)(2,1)} %get-tuple-element.274, s32[]{:T(128)S(6)} %select_n.44), kind=kOutput, calls=%fused_computation.4.clone.1 | convolution fusion | flops 538968064 | bytes 13631620 | tf_op jit(solution)/shard_map/while/body/tij,tjf->tif/dot_general | solution.py:36
  122.4 11.7 %scatter_fusion = f32[8,128,512]{2,1,0:T(8,128)S(1)} fusion(f32[8,128,512]{2,1,0:T(8,128)S(1)} %get-tuple-element.259, s32[32]{0:T(128)S(1)} %get-tuple-element.234, f32[32,128,512]{2,1,0:T(8,128)} %broadcast_multiply_fusion.5), kind=kCustom, calls=%fused_computation.2.clone.1 | custom fusion | flops 2097152 | bytes 25165952 | tf_op jit(solution)/shard_map/while/body/scatter-add | solution.py:39
  139.3 7.0 %broadcast_multiply_fusion.5 = f32[32,128,512]{2,1,0:T(8,128)} fusion(f32[32]{0:T(128)S(1)} %compare_convert_fusion.3, bf16[32,128,512]{2,1,0:T(8,128)(2,1)} %gather_fusion, bf16[256,128,128]{2,1,0:T(8,128)(2,1)} %get-tuple-element.274, s32[]{:T(128)S(6)} %select_n.44), kind=kOutput, calls=%fused_computation.4.clone.1 | convolution fusion | flops 538968064 | bytes 13631620 | tf_op jit(solution)/shard_map/while/body/tij,tjf->tif/dot_general | solution.py:36
  146.3 11.8 %scatter_fusion = f32[8,128,512]{2,1,0:T(8,128)S(1)} fusion(f32[8,128,512]{2,1,0:T(8,128)S(1)} %get-tuple-element.259, s32[32]{0:T(128)S(1)} %get-tuple-element.234, f32[32,128,512]{2,1,0:T(8,128)} %broadcast_multiply_fusion.5), kind=kCustom, calls=%fused_computation.2.clone.1 | custom fusion | flops 2097152 | bytes 25165952 | tf_op jit(solution)/shard_map/while/body/scatter-add | solution.py:39
  158.1 87.7 %all-reduce.4 = bf16[1024,512]{1,0:T(8,128)(2,1)} all-reduce(f32[1024,512]{1,0:T(8,128)S(1)} %bitcast.16), channel_id=1, replica_groups=mesh['node'=8,'rep'=4] {'rep'}, use_global_device_ids=true, to_apply=%region_3.4 | all-reduce | flops 524288 | bytes 3145728 | tf_op jit(solution)/shard_map/psum | solution.py:63
  245.8 5.3 fusion.6
  256.8 117.3 %while.21 = (s32[]{:T(128)}, f32[16,128,512]{2,1,0:T(8,128)}, s32[]{:T(128)}, s32[256]{0:T(256)S(1)}, bf16[256,128,128]{2,1,0:T(8,128)(2,1)}, /*index=5*/s32[256...) while((s32[]{:T(128)}, f32[16,128,512]{2,1,0:T(8,128)}, ...), condition=%wide.region_7.8_spmd, body=%wide.region_5.7_spmd.sunk | while | flops 541066688 | bytes 47191480 | solution.py:41
  260.3 7.3 %broadcast_multiply_fusion.6 = f32[32,128,512]{2,1,0:T(8,128)} fusion(f32[32]{0:T(128)S(1)} %and_select_fusion.2, bf16[32,128,512]{2,1,0:T(8,128)(2,1)} %gather_fusion.1, bf16[256,128,128]{2,1,0:T(8,128)(2,1)} %get-tuple-element.310, s32[]{:T(128)S(6)} %select_n.46), kind=kOutput, calls=%fused_computation.11.clone.1 | convolution fusion | flops 538968064 | bytes 13631620 | tf_op jit(solution)/shard_map/while/body/tji,tjf->tif/dot_general | solution.py:32
  267.6 18.4 %scatter_fusion.1 = f32[16,128,512]{2,1,0:T(8,128)} fusion(f32[16,128,512]{2,1,0:T(8,128)} %get-tuple-element.295, s32[32]{0:T(128)S(1)} %get-tuple-element.244, f32[32,128,512]{2,1,0:T(8,128)} %broadcast_multiply_fusion.6), kind=kCustom, calls=%fused_computation.3.clone.1 | custom fusion | flops 2097152 | bytes 25165952 | tf_op jit(solution)/shard_map/while/body/scatter-add | solution.py:35
  289.5 7.3 %broadcast_multiply_fusion.6 = f32[32,128,512]{2,1,0:T(8,128)} fusion(f32[32]{0:T(128)S(1)} %and_select_fusion.2, bf16[32,128,512]{2,1,0:T(8,128)(2,1)} %gather_fusion.1, bf16[256,128,128]{2,1,0:T(8,128)(2,1)} %get-tuple-element.310, s32[]{:T(128)S(6)} %select_n.46), kind=kOutput, calls=%fused_computation.11.clone.1 | convolution fusion | flops 538968064 | bytes 13631620 | tf_op jit(solution)/shard_map/while/body/tji,tjf->tif/dot_general | solution.py:32
  296.8 18.7 %scatter_fusion.1 = f32[16,128,512]{2,1,0:T(8,128)} fusion(f32[16,128,512]{2,1,0:T(8,128)} %get-tuple-element.295, s32[32]{0:T(128)S(1)} %get-tuple-element.244, f32[32,128,512]{2,1,0:T(8,128)} %broadcast_multiply_fusion.6), kind=kCustom, calls=%fused_computation.3.clone.1 | custom fusion | flops 2097152 | bytes 25165952 | tf_op jit(solution)/shard_map/while/body/scatter-add | solution.py:35
  319.0 7.3 %broadcast_multiply_fusion.6 = f32[32,128,512]{2,1,0:T(8,128)} fusion(f32[32]{0:T(128)S(1)} %and_select_fusion.2, bf16[32,128,512]{2,1,0:T(8,128)(2,1)} %gather_fusion.1, bf16[256,128,128]{2,1,0:T(8,128)(2,1)} %get-tuple-element.310, s32[]{:T(128)S(6)} %select_n.46), kind=kOutput, calls=%fused_computation.11.clone.1 | convolution fusion | flops 538968064 | bytes 13631620 | tf_op jit(solution)/shard_map/while/body/tji,tjf->tif/dot_general | solution.py:32
  326.3 18.3 %scatter_fusion.1 = f32[16,128,512]{2,1,0:T(8,128)} fusion(f32[16,128,512]{2,1,0:T(8,128)} %get-tuple-element.295, s32[32]{0:T(128)S(1)} %get-tuple-element.244, f32[32,128,512]{2,1,0:T(8,128)} %broadcast_multiply_fusion.6), kind=kCustom, calls=%fused_computation.3.clone.1 | custom fusion | flops 2097152 | bytes 25165952 | tf_op jit(solution)/shard_map/while/body/scatter-add | solution.py:35
  348.2 7.3 %broadcast_multiply_fusion.6 = f32[32,128,512]{2,1,0:T(8,128)} fusion(f32[32]{0:T(128)S(1)} %and_select_fusion.2, bf16[32,128,512]{2,1,0:T(8,128)(2,1)} %gather_fusion.1, bf16[256,128,128]{2,1,0:T(8,128)(2,1)} %get-tuple-element.310, s32[]{:T(128)S(6)} %select_n.46), kind=kOutput, calls=%fused_computation.11.clone.1 | convolution fusion | flops 538968064 | bytes 13631620 | tf_op jit(solution)/shard_map/while/body/tji,tjf->tif/dot_general | solution.py:32
  355.5 18.5 %scatter_fusion.1 = f32[16,128,512]{2,1,0:T(8,128)} fusion(f32[16,128,512]{2,1,0:T(8,128)} %get-tuple-element.295, s32[32]{0:T(128)S(1)} %get-tuple-element.244, f32[32,128,512]{2,1,0:T(8,128)} %broadcast_multiply_fusion.6), kind=kCustom, calls=%fused_computation.3.clone.1 | custom fusion | flops 2097152 | bytes 25165952 | tf_op jit(solution)/shard_map/while/body/scatter-add | solution.py:35
  379.9 49.0 %all-reduce.3.cloned.1.call-done = f32[512,512]{1,0:T(8,128)} async-done(((f32[512,512]{1,0:T(8,128)}), f32[512,512]{1,0:T(8,128)}) %all-reduce.3.cloned.1.call-update) | async-done | bytes 1048592 | tf_op jit(solution)/shard_map/psum | solution.py:74
  431.2 173.9 %reduce-scatter.2.cloned.1.call-done = bf16[256,512]{1,0:T(8,128)(2,1)} async-done(((bf16[2048,512]{1,0:T(8,128)(2,1)}), bf16[256,512]{1,0:T(8,128)(2,1)}) %reduce-scatter.2.cloned.1.call-update) | async-done | bytes 262160 | tf_op jit(solution)/shard_map/reduce_scatter | solution.py:79
  (53 shorter events, 45.8 us)
Async XLA Ops:
  7.2 238.7 %copy-start = (bf16[512,512]{1,0:T(8,128)(2,1)S(1)}, bf16[512,512]{1,0:T(8,128)(2,1)}, u32[]{:S(2)}) copy-start(bf16[512,512]{1,0:T(8,128)(2,1)} %param.12) | copy-start | bytes 1572868
  7.2 55.1 %copy-start.1 = (s32[256]{0:T(256)S(1)}, s32[256]{0:T(256)}, u32[]{:S(2)}) copy-start(s32[256]{0:T(256)} %param.16) | copy-start | bytes 3076
  7.2 55.1 %copy-start.2 = (s32[256]{0:T(256)S(1)}, s32[256]{0:T(256)}, u32[]{:S(2)}) copy-start(s32[256]{0:T(256)} %param.15) | copy-start | bytes 3076
  7.2 54.8 %all-gather.3.cloned.1.call-start = ((), (), s32[]{:S(2)}) async-start(), calls=%async_computation.1 | async-start | bytes 2359296 | tf_op jit(solution)/shard_map/all_gather | solution.py:50
  7.9 237.9 %all-gather.5.cloned.1.call-start = ((), (), s32[]{:S(2)}) async-start(), calls=%async_computation.2 | async-start | bytes 1310720 | tf_op jit(solution)/shard_map/all_gather | solution.py:64
  8.7 420.2 %all-reduce.3.cloned.1.call-start = ((), (), s32[]{:S(2)}) async-start(), calls=%async_computation.3 | async-start | bytes 2097152 | tf_op jit(solution)/shard_map/psum | solution.py:74
  254.2 350.8 %reduce-scatter.2.cloned.1.call-start = ((), (), s32[]{:S(2)}) async-start(), calls=%async_computation.4 | async-start | bytes 2359296 | tf_op jit(solution)/shard_map/reduce_scatter | solution.py:79
Sparse Core Ops, SparseCore 0:
  10.1 51.7 all-gather.2
  63.5 15.2 all-gather.4
  254.3 174.4 all-reduce.2
  432.8 172.1 reduce-scatter.1
where the time goes:
time: 614 us; the launch traced here: 612 us
  waiting for transfers between devices  277 us (45%)
  other arithmetic  135 us (22%)
  blocking collectives  87.7 us (14%)
  matrix products  65.7 us (11%)
  local copies, waits for them, and re-layouts  31.2 us (5%)
  between operations  14.5 us (2%)
    reduce_scatter x1, waiting for transfers between devices, local(): lax.psum_scatter(contributions.reshape(-1, feature_width).astype(jnp.bflo...  174 us
    psum x1, blocking collectives, local(): aggregate_all = lax.psum(partial_value, 'rep').astype(jnp.bfloat16)  87.7 us
    scatter-add x4, other arithmetic, one_turn(): return totals.at[placed].add(product * (slot_mask * inside)[:, None, None])  73.9 us
    all_gather x1, waiting for transfers between devices, local(): gathered = lax.all_gather(features, 'node', axis=0, tiled=True)  52.6 us
    psum x1, waiting for transfers between devices, local(): weight_grad = lax.psum(weight_term, ('node', 'rep')) * scale  49 us
    scatter-add x4, other arithmetic, one_turn(): return totals.at[rows_here].add(product * slot_mask[:, None, None])  47.1 us
    dot_general x4, matrix products, one_turn(): jnp.einsum('tji,tjf->tif', values, sources[rows_here], preferred_element_...  29.1 us
    dot_general x4, matrix products, one_turn(): jnp.einsum('tij,tjf->tif', values, sources[cols_here], preferred_element_...  28.2 us
  transfers between devices with their start and end apart: 4, of which 3 were waited for; matrix products, arithmetic and copies ran while one was open for 37% of the time, Pallas kernels for 0%

commit v1 on v0

--- a/solution.py
+++ b/solution.py
@@ -71,7 +71,7 @@
     own_grad = lax.dynamic_slice_in_dim(grad_all, offset, rows_quarter, 0)
     weight_term = jnp.dot(own_aggregate.T, own_grad, preferred_element_type=jnp.float32)
     output_rows = lax.dynamic_slice_in_dim(activated, offset, rows_quarter, 0).astype(jnp.bfloat16)
-    weight_grad = lax.psum(weight_term, ("node", "rep")) * scale
+    weight_grad = lax.psum(lax.psum(weight_term, "rep"), "node") * scale
     grad_blocks = full_grad.reshape(block_count, TB, feature_width)
     contributions = apply_tiles(
         tile_values, tile_row, tile_col, tile_count, grad_blocks, source_blocks.shape, True, 0

time: 614 us -> 647 us (1.054)
  waiting for transfers between devices: 277 us -> 310 us
    psum x1 -> x2, waiting for transfers between devices: 49 us -> 79.5 us  [local(): weight_grad = lax.psum(lax.psum(weight_term, 'rep'), 'node') * scale]
  transfers between devices with their start and end apart: 4 -> 5, of which waited for: 3 -> 3; matrix products, arithmetic and copies ran while one was open for 37% -> 35% of each run, Pallas kernels for 0% -> 0%
where the time goes in v1:
time: 647 us; the launch traced here: 645 us
  waiting for transfers between devices  310 us (48%)
  other arithmetic  135 us (21%)
  blocking collectives  87.7 us (14%)
  matrix products  65.7 us (10%)
  local copies, waits for them, and re-layouts  31.3 us (5%)
  between operations  14.5 us (2%)
    reduce_scatter x1, waiting for transfers between devices, local(): lax.psum_scatter(contributions.reshape(-1, feature_width).astype(jnp.bflo...  176 us
    psum x1, blocking collectives, local(): aggregate_all = lax.psum(partial_value, 'rep').astype(jnp.bfloat16)  87.7 us
    psum x2, waiting for transfers between devices, local(): weight_grad = lax.psum(lax.psum(weight_term, 'rep'), 'node') * scale  79.5 us
    scatter-add x4, other arithmetic, one_turn(): return totals.at[placed].add(product * (slot_mask * inside)[:, None, None])  73.8 us
    all_gather x1, waiting for transfers between devices, local(): gathered = lax.all_gather(features, 'node', axis=0, tiled=True)  52.6 us
    scatter-add x4, other arithmetic, one_turn(): return totals.at[rows_here].add(product * slot_mask[:, None, None])  47.1 us
    dot_general x4, matrix products, one_turn(): jnp.einsum('tji,tjf->tif', values, sources[rows_here], preferred_element_...  29.2 us
    dot_general x4, matrix products, one_turn(): jnp.einsum('tij,tjf->tif', values, sources[cols_here], preferred_element_...  28.2 us
  transfers between devices with their start and end apart: 5, of which 3 were waited for; matrix products, arithmetic and copies ran while one was open for 35% of the time, Pallas kernels for 0%

profile of v1, /device:TPU:0, one launch (start us, length us, event | category | flops | bytes accessed | tf_op | source)
XLA Modules:
  0.0 644.5 jit_solution(5589147025536534071)
XLA Ops:
  9.4 52.6 %all-gather.3.cloned.1.call-done = bf16[2048,512]{1,0:T(8,128)(2,1)} async-done(((bf16[256,512]{1,0:T(8,128)(2,1)}), bf16[2048,512]{1,0:T(8,128)(2,1)}) %all-gather.3.cloned.1.call-update) | async-done | bytes 2097168 | tf_op jit(solution)/shard_map/all_gather | solution.py:50
  62.3 95.9 %while.20 = (s32[]{:T(128)}, f32[8,128,512]{2,1,0:T(8,128)S(1)}, s32[]{:T(128)}, s32[256]{0:T(256)S(1)}, bf16[256,128,128]{2,1,0:T(8,128)(2,1)}, /*index=5*/s32[...) while((s32[]{:T(128)}, f32[8,128,512]{2,1,0:T(8,128)S(1)}, ...), condition=%wide.region_2.3_spmd, body=%wide.region_0.2_spmd.sunk | while | flops 541066560 | bytes 47191344 | solution.py:41
  63.0 4.4 gather_fusion
  67.4 7.2 %broadcast_multiply_fusion.5 = f32[32,128,512]{2,1,0:T(8,128)} fusion(f32[32]{0:T(128)S(1)} %compare_convert_fusion.3, bf16[32,128,512]{2,1,0:T(8,128)(2,1)} %gather_fusion, bf16[256,128,128]{2,1,0:T(8,128)(2,1)} %get-tuple-element.274, s32[]{:T(128)S(6)} %select_n.44), kind=kOutput, calls=%fused_computation.4.clone.1 | convolution fusion | flops 538968064 | bytes 13631620 | tf_op jit(solution)/shard_map/while/body/tij,tjf->tif/dot_general | solution.py:36
  74.6 11.8 %scatter_fusion = f32[8,128,512]{2,1,0:T(8,128)S(1)} fusion(f32[8,128,512]{2,1,0:T(8,128)S(1)} %get-tuple-element.259, s32[32]{0:T(128)S(1)} %get-tuple-element.234, f32[32,128,512]{2,1,0:T(8,128)} %broadcast_multiply_fusion.5), kind=kCustom, calls=%fused_computation.2.clone.1 | custom fusion | flops 2097152 | bytes 25165952 | tf_op jit(solution)/shard_map/while/body/scatter-add | solution.py:39
  91.5 7.0 %broadcast_multiply_fusion.5 = f32[32,128,512]{2,1,0:T(8,128)} fusion(f32[32]{0:T(128)S(1)} %compare_convert_fusion.3, bf16[32,128,512]{2,1,0:T(8,128)(2,1)} %gather_fusion, bf16[256,128,128]{2,1,0:T(8,128)(2,1)} %get-tuple-element.274, s32[]{:T(128)S(6)} %select_n.44), kind=kOutput, calls=%fused_computation.4.clone.1 | convolution fusion | flops 538968064 | bytes 13631620 | tf_op jit(solution)/shard_map/while/body/tij,tjf->tif/dot_general | solution.py:36
  98.5 11.8 %scatter_fusion = f32[8,128,512]{2,1,0:T(8,128)S(1)} fusion(f32[8,128,512]{2,1,0:T(8,128)S(1)} %get-tuple-element.259, s32[32]{0:T(128)S(1)} %get-tuple-element.234, f32[32,128,512]{2,1,0:T(8,128)} %broadcast_multiply_fusion.5), kind=kCustom, calls=%fused_computation.2.clone.1 | custom fusion | flops 2097152 | bytes 25165952 | tf_op jit(solution)/shard_map/while/body/scatter-add | solution.py:39
  115.4 7.0 %broadcast_multiply_fusion.5 = f32[32,128,512]{2,1,0:T(8,128)} fusion(f32[32]{0:T(128)S(1)} %compare_convert_fusion.3, bf16[32,128,512]{2,1,0:T(8,128)(2,1)} %gather_fusion, bf16[256,128,128]{2,1,0:T(8,128)(2,1)} %get-tuple-element.274, s32[]{:T(128)S(6)} %select_n.44), kind=kOutput, calls=%fused_computation.4.clone.1 | convolution fusion | flops 538968064 | bytes 13631620 | tf_op jit(solution)/shard_map/while/body/tij,tjf->tif/dot_general | solution.py:36
  122.4 11.7 %scatter_fusion = f32[8,128,512]{2,1,0:T(8,128)S(1)} fusion(f32[8,128,512]{2,1,0:T(8,128)S(1)} %get-tuple-element.259, s32[32]{0:T(128)S(1)} %get-tuple-element.234, f32[32,128,512]{2,1,0:T(8,128)} %broadcast_multiply_fusion.5), kind=kCustom, calls=%fused_computation.2.clone.1 | custom fusion | flops 2097152 | bytes 25165952 | tf_op jit(solution)/shard_map/while/body/scatter-add | solution.py:39
  139.3 7.0 %broadcast_multiply_fusion.5 = f32[32,128,512]{2,1,0:T(8,128)} fusion(f32[32]{0:T(128)S(1)} %compare_convert_fusion.3, bf16[32,128,512]{2,1,0:T(8,128)(2,1)} %gather_fusion, bf16[256,128,128]{2,1,0:T(8,128)(2,1)} %get-tuple-element.274, s32[]{:T(128)S(6)} %select_n.44), kind=kOutput, calls=%fused_computation.4.clone.1 | convolution fusion | flops 538968064 | bytes 13631620 | tf_op jit(solution)/shard_map/while/body/tij,tjf->tif/dot_general | solution.py:36
  146.3 11.8 %scatter_fusion = f32[8,128,512]{2,1,0:T(8,128)S(1)} fusion(f32[8,128,512]{2,1,0:T(8,128)S(1)} %get-tuple-element.259, s32[32]{0:T(128)S(1)} %get-tuple-element.234, f32[32,128,512]{2,1,0:T(8,128)} %broadcast_multiply_fusion.5), kind=kCustom, calls=%fused_computation.2.clone.1 | custom fusion | flops 2097152 | bytes 25165952 | tf_op jit(solution)/shard_map/while/body/scatter-add | solution.py:39
  158.1 87.7 %all-reduce.7 = bf16[1024,512]{1,0:T(8,128)(2,1)} all-reduce(f32[1024,512]{1,0:T(8,128)S(1)} %bitcast.16), channel_id=1, replica_groups=mesh['node'=8,'rep'=4] {'rep'}, use_global_device_ids=true, to_apply=%region_3.4 | all-reduce | flops 524288 | bytes 3145728 | tf_op jit(solution)/shard_map/psum | solution.py:63
  245.8 5.3 fusion.6
  254.2 79.5 %all-reduce.4.cloned.1.call-done = f32[512,512]{1,0:T(8,128)} async-done(((f32[512,512]{1,0:T(8,128)}), f32[512,512]{1,0:T(8,128)}) %all-reduce.4.cloned.1.call-update) | async-done | bytes 1048592 | tf_op jit(solution)/shard_map/psum | solution.py:74
  336.3 117.3 %while.21 = (s32[]{:T(128)}, f32[16,128,512]{2,1,0:T(8,128)}, s32[]{:T(128)}, s32[256]{0:T(256)S(1)}, bf16[256,128,128]{2,1,0:T(8,128)(2,1)}, /*index=5*/s32[256...) while((s32[]{:T(128)}, f32[16,128,512]{2,1,0:T(8,128)}, ...), condition=%wide.region_8.9_spmd, body=%wide.region_6.8_spmd.sunk | while | flops 541066688 | bytes 47191480 | solution.py:41
  339.8 7.3 %broadcast_multiply_fusion.6 = f32[32,128,512]{2,1,0:T(8,128)} fusion(f32[32]{0:T(128)S(1)} %and_select_fusion.2, bf16[32,128,512]{2,1,0:T(8,128)(2,1)} %gather_fusion.1, bf16[256,128,128]{2,1,0:T(8,128)(2,1)} %get-tuple-element.310, s32[]{:T(128)S(6)} %select_n.46), kind=kOutput, calls=%fused_computation.11.clone.1 | convolution fusion | flops 538968064 | bytes 13631620 | tf_op jit(solution)/shard_map/while/body/tji,tjf->tif/dot_general | solution.py:32
  347.1 18.5 %scatter_fusion.1 = f32[16,128,512]{2,1,0:T(8,128)} fusion(f32[16,128,512]{2,1,0:T(8,128)} %get-tuple-element.295, s32[32]{0:T(128)S(1)} %get-tuple-element.244, f32[32,128,512]{2,1,0:T(8,128)} %broadcast_multiply_fusion.6), kind=kCustom, calls=%fused_computation.3.clone.1 | custom fusion | flops 2097152 | bytes 25165952 | tf_op jit(solution)/shard_map/while/body/scatter-add | solution.py:35
  369.2 7.3 %broadcast_multiply_fusion.6 = f32[32,128,512]{2,1,0:T(8,128)} fusion(f32[32]{0:T(128)S(1)} %and_select_fusion.2, bf16[32,128,512]{2,1,0:T(8,128)(2,1)} %gather_fusion.1, bf16[256,128,128]{2,1,0:T(8,128)(2,1)} %get-tuple-element.310, s32[]{:T(128)S(6)} %select_n.46), kind=kOutput, calls=%fused_computation.11.clone.1 | convolution fusion | flops 538968064 | bytes 13631620 | tf_op jit(solution)/shard_map/while/body/tji,tjf->tif/dot_general | solution.py:32
  376.5 18.6 %scatter_fusion.1 = f32[16,128,512]{2,1,0:T(8,128)} fusion(f32[16,128,512]{2,1,0:T(8,128)} %get-tuple-element.295, s32[32]{0:T(128)S(1)} %get-tuple-element.244, f32[32,128,512]{2,1,0:T(8,128)} %broadcast_multiply_fusion.6), kind=kCustom, calls=%fused_computation.3.clone.1 | custom fusion | flops 2097152 | bytes 25165952 | tf_op jit(solution)/shard_map/while/body/scatter-add | solution.py:35
  398.7 7.4 %broadcast_multiply_fusion.6 = f32[32,128,512]{2,1,0:T(8,128)} fusion(f32[32]{0:T(128)S(1)} %and_select_fusion.2, bf16[32,128,512]{2,1,0:T(8,128)(2,1)} %gather_fusion.1, bf16[256,128,128]{2,1,0:T(8,128)(2,1)} %get-tuple-element.310, s32[]{:T(128)S(6)} %select_n.46), kind=kOutput, calls=%fused_computation.11.clone.1 | convolution fusion | flops 538968064 | bytes 13631620 | tf_op jit(solution)/shard_map/while/body/tji,tjf->tif/dot_general | solution.py:32
  406.1 18.2 %scatter_fusion.1 = f32[16,128,512]{2,1,0:T(8,128)} fusion(f32[16,128,512]{2,1,0:T(8,128)} %get-tuple-element.295, s32[32]{0:T(128)S(1)} %get-tuple-element.244, f32[32,128,512]{2,1,0:T(8,128)} %broadcast_multiply_fusion.6), kind=kCustom, calls=%fused_computation.3.clone.1 | custom fusion | flops 2097152 | bytes 25165952 | tf_op jit(solution)/shard_map/while/body/scatter-add | solution.py:35
  427.9 7.3 %broadcast_multiply_fusion.6 = f32[32,128,512]{2,1,0:T(8,128)} fusion(f32[32]{0:T(128)S(1)} %and_select_fusion.2, bf16[32,128,512]{2,1,0:T(8,128)(2,1)} %gather_fusion.1, bf16[256,128,128]{2,1,0:T(8,128)(2,1)} %get-tuple-element.310, s32[]{:T(128)S(6)} %select_n.46), kind=kOutput, calls=%fused_computation.11.clone.1 | convolution fusion | flops 538968064 | bytes 13631620 | tf_op jit(solution)/shard_map/while/body/tji,tjf->tif/dot_general | solution.py:32
  435.2 18.5 %scatter_fusion.1 = f32[16,128,512]{2,1,0:T(8,128)} fusion(f32[16,128,512]{2,1,0:T(8,128)} %get-tuple-element.295, s32[32]{0:T(128)S(1)} %get-tuple-element.244, f32[32,128,512]{2,1,0:T(8,128)} %broadcast_multiply_fusion.6), kind=kCustom, calls=%fused_computation.3.clone.1 | custom fusion | flops 2097152 | bytes 25165952 | tf_op jit(solution)/shard_map/while/body/scatter-add | solution.py:35
  461.7 176.2 %reduce-scatter.2.cloned.1.call-done = bf16[256,512]{1,0:T(8,128)(2,1)} async-done(((bf16[2048,512]{1,0:T(8,128)(2,1)}), bf16[256,512]{1,0:T(8,128)(2,1)}) %reduce-scatter.2.cloned.1.call-update) | async-done | bytes 262160 | tf_op jit(solution)/shard_map/reduce_scatter | solution.py:79
  (56 shorter events, 45.8 us)
Async XLA Ops:
  7.2 238.7 %copy-start = (bf16[512,512]{1,0:T(8,128)(2,1)S(1)}, bf16[512,512]{1,0:T(8,128)(2,1)}, u32[]{:S(2)}) copy-start(bf16[512,512]{1,0:T(8,128)(2,1)} %param.12) | copy-start | bytes 1572868
  7.2 55.1 %copy-start.1 = (s32[256]{0:T(256)S(1)}, s32[256]{0:T(256)}, u32[]{:S(2)}) copy-start(s32[256]{0:T(256)} %param.16) | copy-start | bytes 3076
  7.2 55.1 %copy-start.2 = (s32[256]{0:T(256)S(1)}, s32[256]{0:T(256)}, u32[]{:S(2)}) copy-start(s32[256]{0:T(256)} %param.15) | copy-start | bytes 3076
  7.2 54.8 %all-gather.3.cloned.1.call-start = ((), (), s32[]{:S(2)}) async-start(), calls=%async_computation.1 | async-start | bytes 2359296 | tf_op jit(solution)/shard_map/all_gather | solution.py:50
  7.9 237.9 %all-gather.5.cloned.1.call-start = ((), (), s32[]{:S(2)}) async-start(), calls=%async_computation.2 | async-start | bytes 1310720 | tf_op jit(solution)/shard_map/all_gather | solution.py:64
  8.7 325.0 %all-reduce.4.cloned.1.call-start = ((), (), s32[]{:S(2)}) async-start(), calls=%async_computation.3 | async-start | bytes 2097152 | tf_op jit(solution)/shard_map/psum | solution.py:74
  253.4 206.0 %all-reduce.6.cloned.1.call-start = ((), (), s32[]{:S(2)}) async-start(), calls=%async_computation.4 | async-start | bytes 2097152 | tf_op jit(solution)/shard_map/psum | solution.py:74
  333.7 304.2 %reduce-scatter.2.cloned.1.call-start = ((), (), s32[]{:S(2)}) async-start(), calls=%async_computation.5 | async-start | bytes 2359296 | tf_op jit(solution)/shard_map/reduce_scatter | solution.py:79
Sparse Core Ops, SparseCore 0:
  10.1 51.7 all-gather.2
  63.5 15.2 all-gather.4
  253.6 80.1 all-reduce.3
  337.1 78.7 all-reduce.5
  457.6 180.3 reduce-scatter.1
